TPU v7x, 256 devices: a whole 4x4x8 slice. The times are simulated.
256 devices in a mesh: pipe: 16 (over y, x), dp: 16 (over z, core).
Axes of the slice: x: 4, y: 4, z: 8, core: 2. Of those that a mesh axis runs over, the one named last changes fastest.
Arguments:
- first_input: bfloat16 [4, 1024, 8192], P(None, 'dp'), may hold values from -6 to 6
- section_gain: float32 [16, 8192], P('pipe'), may hold values from 0.5 to 1.5
- value_panel: bfloat16 [16, 8192, 512], P('pipe', 'dp'), may hold values from -0.0625 to 0.0625
- output_panel: bfloat16 [16, 512, 8192], P('pipe', 'dp'), may hold values from -0.125 to 0.125
- value_tiles: bfloat16 [16, 32, 4096], P('pipe', 'dp'), may hold values from -0.1875 to 0.1875
- output_tiles: bfloat16 [16, 32, 4096], P('pipe', 'dp'), may hold values from -0.375 to 0.375
- value_blocks: int32 [16, 32], P('pipe'), may hold values from 0 to 1023, as said below
- output_blocks: int32 [16, 32], P('pipe'), may hold values from 0 to 1023, as said below
- upstream: bfloat16 [16, 4, 1024, 8192], P('pipe', None, 'dp'), may hold values from -0.08984375 to 0.08984375
Outputs:
- value_tile_grads: float32 [16, 32, 4096], P('pipe', 'dp')
- output_tile_grads: float32 [16, 32, 4096], P('pipe', 'dp')
Inputs may be any that keep to these rules, and one draw needn't show every extreme that they name: `value_blocks`: the 32 block numbers of one section and one matrix are distinct; in section 0 both 0 and the largest block number occur. `output_blocks`: the 32 block numbers of one section and one matrix are distinct; in section 0 both 0 and the largest block number occur.
All inputs are finite; a program needn't handle non-finite values.
Results may differ from a plain program's by a relative error of at most 0.025.
Values may be sent and summed in bfloat16 or wider, within the bound.
A program may use at most 192 MiB of HBM per device.

v0:
```python
import jax
import jax.numpy as jnp
from jax import lax
from jax.sharding import PartitionSpec as P

BLK = 64


NORM_EPS = 1e-05


def from_behind(value, axis, steps):
    count = lax.axis_size(axis)
    initial, last = (max(0, -steps), min(count, count - steps))
    return lax.ppermute(value, axis, [(source, source + steps) for source in range(initial, last)])


def effective_panel(panel, delta, blocks):
    col_count = panel.shape[1] // BLK
    blocked = panel.reshape(panel.shape[0] // BLK, BLK, col_count, BLK)
    blocked = blocked.at[blocks // col_count, :, blocks % col_count, :].add(
        delta.reshape(blocks.shape[0], BLK, BLK)
    )
    return blocked.reshape(panel.shape)


def section_forward(hidden, scaling, value_eff, output_eff):
    widened = hidden.astype(jnp.float32)
    inverse_rms = lax.rsqrt(jnp.mean(widened * widened, axis=-1, keepdims=True) + NORM_EPS)
    normed = (widened * inverse_rms * scaling).astype(jnp.bfloat16)
    values = jnp.dot(normed, value_eff, preferred_element_type=jnp.float32).astype(jnp.bfloat16)
    mixed = jnp.dot(values, output_eff, preferred_element_type=jnp.float32)
    following = (widened + mixed).astype(jnp.bfloat16)
    return (normed, values, following)


def back_value(incoming, output_eff):
    product = lax.dot_general(
        incoming, output_eff, (((1,), (1,)), ((), ())), preferred_element_type=jnp.float32
    )
    return product.astype(jnp.bfloat16)


def tile_products(acts, grads, blocks, col_count):
    count = acts.shape[0]
    left_blocks = acts.reshape(count, acts.shape[1] // BLK, BLK)[:, blocks // col_count, :]
    right_blocks = grads.reshape(count, grads.shape[1] // BLK, BLK)[:, blocks % col_count, :]
    products = jnp.einsum(
        "nka,nkb->kab", left_blocks, right_blocks, preferred_element_type=jnp.float32
    )
    return products.reshape(blocks.shape[0], BLK * BLK)


def shards(
    first_input,
    section_gain,
    value_panel,
    output_panel,
    value_tiles,
    output_tiles,
    value_blocks,
    output_blocks,
    upstream,
):
    value_full, output_full, value_delta, output_delta = (
        lax.all_gather(value_panel, "dp", axis=1, tiled=True),
        lax.all_gather(output_panel, "dp", axis=1, tiled=True),
        lax.all_gather(value_tiles, "dp", axis=1, tiled=True),
        lax.all_gather(output_tiles, "dp", axis=1, tiled=True),
    )
    value_eff = effective_panel(value_full[0], value_delta[0], value_blocks[0])
    output_eff = effective_panel(output_full[0], output_delta[0], output_blocks[0])
    scaling = section_gain[0]
    position = lax.axis_index("pipe")
    sections = lax.axis_size("pipe")
    micro_count = first_input.shape[0]
    token_rows = first_input.shape[1]
    width = first_input.shape[2]
    value_width = value_eff.shape[1]
    incoming_all = upstream[0]
    tile_count = value_blocks.shape[1]
    value_cols = value_width // BLK
    output_cols = width // BLK
    start_store = (
        jnp.zeros((tile_count, BLK * BLK), jnp.float32),
        jnp.zeros((tile_count, BLK * BLK), jnp.float32),
    )

    def record(store, normed, values, value_grad, incoming):
        return (
            store[0] + tile_products(normed, value_grad, value_blocks[0], value_cols),
            store[1] + tile_products(values, incoming, output_blocks[0], output_cols),
        )

    def advance(operands):
        hidden, store, micro_slot = operands
        normed, values, following = section_forward(hidden, scaling, value_eff, output_eff)
        incoming = lax.dynamic_index_in_dim(incoming_all, micro_slot, 0, keepdims=False)
        value_grad = back_value(incoming, output_eff)
        return (following, record(store, normed, values, value_grad, incoming))

    def pause(operands):
        hidden, store, micro_slot = operands
        return (jnp.zeros_like(hidden), store)

    def step(moment, carry):
        arrived, store = carry
        micro_index = moment - position
        active = jnp.logical_and(micro_index >= 0, micro_index < micro_count)
        micro_slot = jnp.clip(micro_index, 0, micro_count - 1)
        fresh_input = lax.dynamic_index_in_dim(first_input, micro_slot, 0, keepdims=False)
        hidden = jnp.where(position == 0, fresh_input, arrived)
        following, store = lax.cond(active, advance, pause, (hidden, store, micro_slot))
        arrived = from_behind(following, "pipe", 1)
        return (arrived, store)

    start_arrived = jnp.zeros((token_rows, width), jnp.bfloat16)
    last_arrived, last_store = lax.fori_loop(
        0, micro_count + sections - 1, step, (start_arrived, start_store)
    )
    partial_value, partial_output = last_store
    value_grads, output_grads = (
        lax.psum_scatter(
            partial_value.astype(jnp.bfloat16), "dp", scatter_dimension=0, tiled=True
        ).astype(jnp.float32),
        lax.psum_scatter(
            partial_output.astype(jnp.bfloat16), "dp", scatter_dimension=0, tiled=True
        ).astype(jnp.float32),
    )
    return (value_grads[None], output_grads[None])


def solution(mesh):
    in_specs = (
        P(None, "dp", None),
        P("pipe", None),
        P("pipe", "dp", None),
        P("pipe", "dp", None),
        P("pipe", "dp", None),
        P("pipe", "dp", None),
        P("pipe", None),
        P("pipe", None),
        P("pipe", None, "dp", None),
    )
    out_specs = (P("pipe", "dp", None), P("pipe", "dp", None))
    return jax.shard_map(shards, mesh=mesh, in_specs=in_specs, out_specs=out_specs, check_vma=False)
```

profile of v0, /device:TPU:31, one launch (start us, length us, event | category | flops | bytes accessed | tf_op | source)
XLA Modules:
  0.0 1778.4 jit_solution(6487063991671305757)
XLA Ops:
  9.4 23.3 %all_gather.13 = bf16[1,32,4096]{2,0,1:T(2,128)(2,1)S(1)} all-gather(bf16[1,2,4096]{2,0,1:T(2,128)(2,1)S(1)} %copy.39), channel_id=1, replica_groups=mesh['pipe'=16,'dp'=16] {'dp'}, dimensions={1}, use_global_device_ids=true | all-gather | bytes 278528 | tf_op jit(solution)/shard_map/all_gather | solution.py:68
  71.9 21.2 %reshape_squeeze.12 = bf16[128,64,8,64]{3,2,1,0:T(8,128)(2,1)} reshape(bf16[1,8192,512]{2,1,0:T(8,128)(2,1)} %all-gather.3.cloned.1.call-done) | data formatting | bytes 16777216 | tf_op jit(solution)/shard_map/reshape;squeeze | solution.py:20
  113.5 20.3 %copy.41 = bf16[128,64,8,64]{3,2,1,0:T(8,128)(2,1)} copy(bf16[128,64,8,64]{3,1,2,0:T(8,128)(2,1)} %scatter_fusion) | data formatting | bytes 16777216 | tf_op jit(solution)/shard_map/scatter-add | solution.py:21
  133.8 22.5 %reshape.554 = bf16[8192,512]{1,0:T(8,128)(2,1)} reshape(bf16[128,64,8,64]{3,2,1,0:T(8,128)(2,1)} %copy.41) | data formatting | bytes 16777216 | tf_op jit(solution)/shard_map/reshape | solution.py:24
  156.3 23.6 %reshape_squeeze.14 = bf16[8,64,128,64]{3,2,1,0:T(8,128)(2,1)} reshape(bf16[1,512,8192]{2,1,0:T(8,128)(2,1)} %all-gather.5.cloned.1.call-done) | data formatting | bytes 16777216 | tf_op jit(solution)/shard_map/reshape;squeeze | solution.py:20
  222.0 22.6 %reshape.555 = bf16[512,8192]{1,0:T(8,128)(2,1)} reshape(bf16[8,64,128,64]{3,2,1,0:T(8,128)(2,1)} %copy.44) | data formatting | bytes 16777216 | tf_op jit(solution)/shard_map/reshape | solution.py:24
  246.4 1399.1 %while.18 = (s32[]{:T(128)}, bf16[64,8192]{1,0:T(8,128)(2,1)S(1)}, f32[32,4096]{1,0:T(8,128)}, f32[32,4096]{1,0:T(8,128)}, s32[]{:T(128)}, /*index=5*/pred[]{:T(...) while((s32[]{:T(128)}, bf16[64,8192]{1,0:T(8,128)(2,1)S(1)}, ...), condition=%wide.region_6.7_spmd, body=%wide.region_2.6_spmd.sunk | while | flops 1650267648 | bytes 59493512 | solution.py:118
  249.1 25.2 %collective-permute-done = bf16[64,8192]{1,0:T(8,128)(2,1)S(1)} collective-permute-done((bf16[64,8192]{1,0:T(8,128)(2,1)}, bf16[64,8192]{1,0:T(8,128)(2,1)S(1)}, u32[]{:S(2)}, u32[]{:S(2)}) %collective-permute-start) | collective-permute-done | bytes 1048608 | tf_op jit(solution)/shard_map/while/body/eval_jaxpr/ppermute | solution.py:15
  276.7 24.4 %collective-permute-done = bf16[64,8192]{1,0:T(8,128)(2,1)S(1)} collective-permute-done((bf16[64,8192]{1,0:T(8,128)(2,1)}, bf16[64,8192]{1,0:T(8,128)(2,1)S(1)}, u32[]{:S(2)}, u32[]{:S(2)}) %collective-permute-start) | collective-permute-done | bytes 1048608 | tf_op jit(solution)/shard_map/while/body/eval_jaxpr/ppermute | solution.py:15
  303.4 23.5 %collective-permute-done = bf16[64,8192]{1,0:T(8,128)(2,1)S(1)} collective-permute-done((bf16[64,8192]{1,0:T(8,128)(2,1)}, bf16[64,8192]{1,0:T(8,128)(2,1)S(1)}, u32[]{:S(2)}, u32[]{:S(2)}) %collective-permute-start) | collective-permute-done | bytes 1048608 | tf_op jit(solution)/shard_map/while/body/eval_jaxpr/ppermute | solution.py:15
  329.3 22.6 %collective-permute-done = bf16[64,8192]{1,0:T(8,128)(2,1)S(1)} collective-permute-done((bf16[64,8192]{1,0:T(8,128)(2,1)}, bf16[64,8192]{1,0:T(8,128)(2,1)S(1)}, u32[]{:S(2)}, u32[]{:S(2)}) %collective-permute-start) | collective-permute-done | bytes 1048608 | tf_op jit(solution)/shard_map/while/body/eval_jaxpr/ppermute | solution.py:15
  354.4 24.5 %collective-permute-done = bf16[64,8192]{1,0:T(8,128)(2,1)S(1)} collective-permute-done((bf16[64,8192]{1,0:T(8,128)(2,1)}, bf16[64,8192]{1,0:T(8,128)(2,1)S(1)}, u32[]{:S(2)}, u32[]{:S(2)}) %collective-permute-start) | collective-permute-done | bytes 1048608 | tf_op jit(solution)/shard_map/while/body/eval_jaxpr/ppermute | solution.py:15
  381.3 23.0 %collective-permute-done = bf16[64,8192]{1,0:T(8,128)(2,1)S(1)} collective-permute-done((bf16[64,8192]{1,0:T(8,128)(2,1)}, bf16[64,8192]{1,0:T(8,128)(2,1)S(1)}, u32[]{:S(2)}, u32[]{:S(2)}) %collective-permute-start) | collective-permute-done | bytes 1048608 | tf_op jit(solution)/shard_map/while/body/eval_jaxpr/ppermute | solution.py:15
  406.7 22.2 %collective-permute-done = bf16[64,8192]{1,0:T(8,128)(2,1)S(1)} collective-permute-done((bf16[64,8192]{1,0:T(8,128)(2,1)}, bf16[64,8192]{1,0:T(8,128)(2,1)S(1)}, u32[]{:S(2)}, u32[]{:S(2)}) %collective-permute-start) | collective-permute-done | bytes 1048608 | tf_op jit(solution)/shard_map/while/body/eval_jaxpr/ppermute | solution.py:15
  431.3 21.3 %collective-permute-done = bf16[64,8192]{1,0:T(8,128)(2,1)S(1)} collective-permute-done((bf16[64,8192]{1,0:T(8,128)(2,1)}, bf16[64,8192]{1,0:T(8,128)(2,1)S(1)}, u32[]{:S(2)}, u32[]{:S(2)}) %collective-permute-start) | collective-permute-done | bytes 1048608 | tf_op jit(solution)/shard_map/while/body/eval_jaxpr/ppermute | solution.py:15
  455.0 20.5 %collective-permute-done = bf16[64,8192]{1,0:T(8,128)(2,1)S(1)} collective-permute-done((bf16[64,8192]{1,0:T(8,128)(2,1)}, bf16[64,8192]{1,0:T(8,128)(2,1)S(1)}, u32[]{:S(2)}, u32[]{:S(2)}) %collective-permute-start) | collective-permute-done | bytes 1048608 | tf_op jit(solution)/shard_map/while/body/eval_jaxpr/ppermute | solution.py:15
  543.2 20.5 %collective-permute-done = bf16[64,8192]{1,0:T(8,128)(2,1)S(1)} collective-permute-done((bf16[64,8192]{1,0:T(8,128)(2,1)}, bf16[64,8192]{1,0:T(8,128)(2,1)S(1)}, u32[]{:S(2)}, u32[]{:S(2)}) %collective-permute-start) | collective-permute-done | bytes 1048608 | tf_op jit(solution)/shard_map/while/body/eval_jaxpr/ppermute | solution.py:15
  566.1 21.0 %collective-permute-done = bf16[64,8192]{1,0:T(8,128)(2,1)S(1)} collective-permute-done((bf16[64,8192]{1,0:T(8,128)(2,1)}, bf16[64,8192]{1,0:T(8,128)(2,1)S(1)}, u32[]{:S(2)}, u32[]{:S(2)}) %collective-permute-start) | collective-permute-done | bytes 1048608 | tf_op jit(solution)/shard_map/while/body/eval_jaxpr/ppermute | solution.py:15
  589.4 775.5 %collective-permute-done = bf16[64,8192]{1,0:T(8,128)(2,1)S(1)} collective-permute-done((bf16[64,8192]{1,0:T(8,128)(2,1)}, bf16[64,8192]{1,0:T(8,128)(2,1)S(1)}, u32[]{:S(2)}, u32[]{:S(2)}) %collective-permute-start) | collective-permute-done | bytes 1048608 | tf_op jit(solution)/shard_map/while/body/eval_jaxpr/ppermute | solution.py:15
  1364.9 52.5 %conditional.2 = (bf16[64,8192]{1,0:T(8,128)(2,1)}, f32[32,4096]{1,0:T(8,128)}, f32[32,4096]{1,0:T(8,128)}) conditional(s32[]{:T(128)} %convert_element_type.62, (f32[32,4096]{1,0:T(8,128)}, f32[32,4096]{1,0:T(8,128)}) %tuple.60, (pred[]{:T(512)}, s32[]{:T(128)}, bf16[4,64,8192]{2,1,0:T(8,128)(2,1)}, bf16[64,8192]{1,0:T(8,128)(2,1)S(1)}, ...), branch_computations={%region_3.3_spmd, %region_4.5_spmd} | conditional | flops 1650267648 | bytes 55298872 | solution.py:113
  1436.6 52.5 %conditional.2 = (bf16[64,8192]{1,0:T(8,128)(2,1)}, f32[32,4096]{1,0:T(8,128)}, f32[32,4096]{1,0:T(8,128)}) conditional(s32[]{:T(128)} %convert_element_type.62, (f32[32,4096]{1,0:T(8,128)}, f32[32,4096]{1,0:T(8,128)}) %tuple.60, (pred[]{:T(512)}, s32[]{:T(128)}, bf16[4,64,8192]{2,1,0:T(8,128)(2,1)}, bf16[64,8192]{1,0:T(8,128)(2,1)S(1)}, ...), branch_computations={%region_3.3_spmd, %region_4.5_spmd} | conditional | flops 1650267648 | bytes 55298872 | solution.py:113
  1507.4 52.5 %conditional.2 = (bf16[64,8192]{1,0:T(8,128)(2,1)}, f32[32,4096]{1,0:T(8,128)}, f32[32,4096]{1,0:T(8,128)}) conditional(s32[]{:T(128)} %convert_element_type.62, (f32[32,4096]{1,0:T(8,128)}, f32[32,4096]{1,0:T(8,128)}) %tuple.60, (pred[]{:T(512)}, s32[]{:T(128)}, bf16[4,64,8192]{2,1,0:T(8,128)(2,1)}, bf16[64,8192]{1,0:T(8,128)(2,1)S(1)}, ...), branch_computations={%region_3.3_spmd, %region_4.5_spmd} | conditional | flops 1650267648 | bytes 55298872 | solution.py:113
  1577.3 52.5 %conditional.2 = (bf16[64,8192]{1,0:T(8,128)(2,1)}, f32[32,4096]{1,0:T(8,128)}, f32[32,4096]{1,0:T(8,128)}) conditional(s32[]{:T(128)} %convert_element_type.62, (f32[32,4096]{1,0:T(8,128)}, f32[32,4096]{1,0:T(8,128)}) %tuple.60, (pred[]{:T(512)}, s32[]{:T(128)}, bf16[4,64,8192]{2,1,0:T(8,128)(2,1)}, bf16[64,8192]{1,0:T(8,128)(2,1)S(1)}, ...), branch_computations={%region_3.3_spmd, %region_4.5_spmd} | conditional | flops 1650267648 | bytes 55298872 | solution.py:113
  1650.3 120.0 %all-reduce.5.cloned.1.call-done = (bf16[32,4096]{1,0:T(8,128)(2,1)}, bf16[32,4096]{1,0:T(8,128)(2,1)}) async-done(((bf16[32,4096]{1,0:T(8,128)(2,1)}, bf16[32,4096]{1,0:T(8,128)(2,1)}), (bf16[32,4096]{1,0:T(8,128)(2,1)}, bf16[32,4096]{1,0:T(8,128)(2,1)})) %all-reduce.5.cloned.1.call-update) | async-done | bytes 524304
  (213 shorter events, 502.0 us)
Async XLA Ops:
  7.2 64.7 %all-gather.3.cloned.1.call-start = ((), (), s32[]{:S(2)}) async-start(), calls=%async_computation | async-start | bytes 8912896 | tf_op jit(solution)/shard_map/all_gather | solution.py:66
  7.9 148.4 %all-gather.5.cloned.1.call-start = ((), (), s32[]{:S(2)}) async-start(), calls=%async_computation.1 | async-start | bytes 8912896 | tf_op jit(solution)/shard_map/all_gather | solution.py:67
  8.6 1761.7 %all-reduce.5.cloned.1.call-start = ((), (), s32[]{:S(2)}) async-start(), calls=%async_computation.2 | async-start | bytes 1048576
  222.0 24.4 %copy-start.2 = (s32[1,32]{1,0:T(1,128)S(1)}, s32[1,32]{1,0:T(1,128)}, u32[]{:S(2)}) copy-start(s32[1,32]{1,0:T(1,128)} %param.20) | copy-start | bytes 388
  246.4 1402.7 %copy-start.3 = (u32[256]{0:T(256)S(1)}, u32[256]{0:T(256)}, u32[]{:S(2)}) copy-start(u32[256]{0:T(256)} %constant.249) | copy-start | bytes 3076
  247.8 26.5 %collective-permute-start = (bf16[64,8192]{1,0:T(8,128)(2,1)}, bf16[64,8192]{1,0:T(8,128)(2,1)S(1)}, u32[]{:S(2)}, u32[]{:S(2)}) collective-permute-start(bf16[64,8192]{1,0:T(8,128)(2,1)} %get-tuple-element.515), channel_id=1, source_target_pairs={{0,16},{16,32},{32,48},{48,64},{64,80},{80,96},{96,112},{112,128},... | collective-permute-start | bytes 3145736 | tf_op jit(solution)/shard_map/while/body/eval_jaxpr/ppermute | solution.py:15
  275.4 25.6 %collective-permute-start = (bf16[64,8192]{1,0:T(8,128)(2,1)}, bf16[64,8192]{1,0:T(8,128)(2,1)S(1)}, u32[]{:S(2)}, u32[]{:S(2)}) collective-permute-start(bf16[64,8192]{1,0:T(8,128)(2,1)} %get-tuple-element.515), channel_id=1, source_target_pairs={{0,16},{16,32},{32,48},{48,64},{64,80},{80,96},{96,112},{112,128},... | collective-permute-start | bytes 3145736 | tf_op jit(solution)/shard_map/while/body/eval_jaxpr/ppermute | solution.py:15
  302.2 24.8 %collective-permute-start = (bf16[64,8192]{1,0:T(8,128)(2,1)}, bf16[64,8192]{1,0:T(8,128)(2,1)S(1)}, u32[]{:S(2)}, u32[]{:S(2)}) collective-permute-start(bf16[64,8192]{1,0:T(8,128)(2,1)} %get-tuple-element.515), channel_id=1, source_target_pairs={{0,16},{16,32},{32,48},{48,64},{64,80},{80,96},{96,112},{112,128},... | collective-permute-start | bytes 3145736 | tf_op jit(solution)/shard_map/while/body/eval_jaxpr/ppermute | solution.py:15
  328.1 23.9 %collective-permute-start = (bf16[64,8192]{1,0:T(8,128)(2,1)}, bf16[64,8192]{1,0:T(8,128)(2,1)S(1)}, u32[]{:S(2)}, u32[]{:S(2)}) collective-permute-start(bf16[64,8192]{1,0:T(8,128)(2,1)} %get-tuple-element.515), channel_id=1, source_target_pairs={{0,16},{16,32},{32,48},{48,64},{64,80},{80,96},{96,112},{112,128},... | collective-permute-start | bytes 3145736 | tf_op jit(solution)/shard_map/while/body/eval_jaxpr/ppermute | solution.py:15
  353.1 25.8 %collective-permute-start = (bf16[64,8192]{1,0:T(8,128)(2,1)}, bf16[64,8192]{1,0:T(8,128)(2,1)S(1)}, u32[]{:S(2)}, u32[]{:S(2)}) collective-permute-start(bf16[64,8192]{1,0:T(8,128)(2,1)} %get-tuple-element.515), channel_id=1, source_target_pairs={{0,16},{16,32},{32,48},{48,64},{64,80},{80,96},{96,112},{112,128},... | collective-permute-start | bytes 3145736 | tf_op jit(solution)/shard_map/while/body/eval_jaxpr/ppermute | solution.py:15
  380.0 24.3 %collective-permute-start = (bf16[64,8192]{1,0:T(8,128)(2,1)}, bf16[64,8192]{1,0:T(8,128)(2,1)S(1)}, u32[]{:S(2)}, u32[]{:S(2)}) collective-permute-start(bf16[64,8192]{1,0:T(8,128)(2,1)} %get-tuple-element.515), channel_id=1, source_target_pairs={{0,16},{16,32},{32,48},{48,64},{64,80},{80,96},{96,112},{112,128},... | collective-permute-start | bytes 3145736 | tf_op jit(solution)/shard_map/while/body/eval_jaxpr/ppermute | solution.py:15
  405.4 23.5 %collective-permute-start = (bf16[64,8192]{1,0:T(8,128)(2,1)}, bf16[64,8192]{1,0:T(8,128)(2,1)S(1)}, u32[]{:S(2)}, u32[]{:S(2)}) collective-permute-start(bf16[64,8192]{1,0:T(8,128)(2,1)} %get-tuple-element.515), channel_id=1, source_target_pairs={{0,16},{16,32},{32,48},{48,64},{64,80},{80,96},{96,112},{112,128},... | collective-permute-start | bytes 3145736 | tf_op jit(solution)/shard_map/while/body/eval_jaxpr/ppermute | solution.py:15
  430.0 22.6 %collective-permute-start = (bf16[64,8192]{1,0:T(8,128)(2,1)}, bf16[64,8192]{1,0:T(8,128)(2,1)S(1)}, u32[]{:S(2)}, u32[]{:S(2)}) collective-permute-start(bf16[64,8192]{1,0:T(8,128)(2,1)} %get-tuple-element.515), channel_id=1, source_target_pairs={{0,16},{16,32},{32,48},{48,64},{64,80},{80,96},{96,112},{112,128},... | collective-permute-start | bytes 3145736 | tf_op jit(solution)/shard_map/while/body/eval_jaxpr/ppermute | solution.py:15
  453.7 21.8 %collective-permute-start = (bf16[64,8192]{1,0:T(8,128)(2,1)}, bf16[64,8192]{1,0:T(8,128)(2,1)S(1)}, u32[]{:S(2)}, u32[]{:S(2)}) collective-permute-start(bf16[64,8192]{1,0:T(8,128)(2,1)} %get-tuple-element.515), channel_id=1, source_target_pairs={{0,16},{16,32},{32,48},{48,64},{64,80},{80,96},{96,112},{112,128},... | collective-permute-start | bytes 3145736 | tf_op jit(solution)/shard_map/while/body/eval_jaxpr/ppermute | solution.py:15
  476.6 20.9 %collective-permute-start = (bf16[64,8192]{1,0:T(8,128)(2,1)}, bf16[64,8192]{1,0:T(8,128)(2,1)S(1)}, u32[]{:S(2)}, u32[]{:S(2)}) collective-permute-start(bf16[64,8192]{1,0:T(8,128)(2,1)} %get-tuple-element.515), channel_id=1, source_target_pairs={{0,16},{16,32},{32,48},{48,64},{64,80},{80,96},{96,112},{112,128},... | collective-permute-start | bytes 3145736 | tf_op jit(solution)/shard_map/while/body/eval_jaxpr/ppermute | solution.py:15
  498.7 20.5 %collective-permute-start = (bf16[64,8192]{1,0:T(8,128)(2,1)}, bf16[64,8192]{1,0:T(8,128)(2,1)S(1)}, u32[]{:S(2)}, u32[]{:S(2)}) collective-permute-start(bf16[64,8192]{1,0:T(8,128)(2,1)} %get-tuple-element.515), channel_id=1, source_target_pairs={{0,16},{16,32},{32,48},{48,64},{64,80},{80,96},{96,112},{112,128},... | collective-permute-start | bytes 3145736 | tf_op jit(solution)/shard_map/while/body/eval_jaxpr/ppermute | solution.py:15
  520.3 20.5 %collective-permute-start = (bf16[64,8192]{1,0:T(8,128)(2,1)}, bf16[64,8192]{1,0:T(8,128)(2,1)S(1)}, u32[]{:S(2)}, u32[]{:S(2)}) collective-permute-start(bf16[64,8192]{1,0:T(8,128)(2,1)} %get-tuple-element.515), channel_id=1, source_target_pairs={{0,16},{16,32},{32,48},{48,64},{64,80},{80,96},{96,112},{112,128},... | collective-permute-start | bytes 3145736 | tf_op jit(solution)/shard_map/while/body/eval_jaxpr/ppermute | solution.py:15
  541.9 21.8 %collective-permute-start = (bf16[64,8192]{1,0:T(8,128)(2,1)}, bf16[64,8192]{1,0:T(8,128)(2,1)S(1)}, u32[]{:S(2)}, u32[]{:S(2)}) collective-permute-start(bf16[64,8192]{1,0:T(8,128)(2,1)} %get-tuple-element.515), channel_id=1, source_target_pairs={{0,16},{16,32},{32,48},{48,64},{64,80},{80,96},{96,112},{112,128},... | collective-permute-start | bytes 3145736 | tf_op jit(solution)/shard_map/while/body/eval_jaxpr/ppermute | solution.py:15
  564.8 22.2 %collective-permute-start = (bf16[64,8192]{1,0:T(8,128)(2,1)}, bf16[64,8192]{1,0:T(8,128)(2,1)S(1)}, u32[]{:S(2)}, u32[]{:S(2)}) collective-permute-start(bf16[64,8192]{1,0:T(8,128)(2,1)} %get-tuple-element.515), channel_id=1, source_target_pairs={{0,16},{16,32},{32,48},{48,64},{64,80},{80,96},{96,112},{112,128},... | collective-permute-start | bytes 3145736 | tf_op jit(solution)/shard_map/while/body/eval_jaxpr/ppermute | solution.py:15
  588.1 776.8 %collective-permute-start = (bf16[64,8192]{1,0:T(8,128)(2,1)}, bf16[64,8192]{1,0:T(8,128)(2,1)S(1)}, u32[]{:S(2)}, u32[]{:S(2)}) collective-permute-start(bf16[64,8192]{1,0:T(8,128)(2,1)} %get-tuple-element.515), channel_id=1, source_target_pairs={{0,16},{16,32},{32,48},{48,64},{64,80},{80,96},{96,112},{112,128},... | collective-permute-start | bytes 3145736 | tf_op jit(solution)/shard_map/while/body/eval_jaxpr/ppermute | solution.py:15
  1417.5 19.1 %collective-permute-start = (bf16[64,8192]{1,0:T(8,128)(2,1)}, bf16[64,8192]{1,0:T(8,128)(2,1)S(1)}, u32[]{:S(2)}, u32[]{:S(2)}) collective-permute-start(bf16[64,8192]{1,0:T(8,128)(2,1)} %get-tuple-element.515), channel_id=1, source_target_pairs={{0,16},{16,32},{32,48},{48,64},{64,80},{80,96},{96,112},{112,128},... | collective-permute-start | bytes 3145736 | tf_op jit(solution)/shard_map/while/body/eval_jaxpr/ppermute | solution.py:15
  1489.1 18.2 %collective-permute-start = (bf16[64,8192]{1,0:T(8,128)(2,1)}, bf16[64,8192]{1,0:T(8,128)(2,1)S(1)}, u32[]{:S(2)}, u32[]{:S(2)}) collective-permute-start(bf16[64,8192]{1,0:T(8,128)(2,1)} %get-tuple-element.515), channel_id=1, source_target_pairs={{0,16},{16,32},{32,48},{48,64},{64,80},{80,96},{96,112},{112,128},... | collective-permute-start | bytes 3145736 | tf_op jit(solution)/shard_map/while/body/eval_jaxpr/ppermute | solution.py:15
  1559.9 17.4 collective-permute-start
  1629.8 15.7 collective-permute-start
  (2 other events, 48.8 us)
Sparse Core Ops, SparseCore 0:
  9.8 62.0 all-gather.2
  73.7 54.3 all-gather.4
  1649.2 121.0 all-reduce.4
where the time goes:
time: 1790 us; the launch traced here: 1780 us
  waiting for transfers between devices  1280 us (72%)
  local copies, waits for them, and re-layouts  285 us (16%)
  matrix products  84.3 us (5%)
  other arithmetic  43.8 us (2%)
  blocking collectives  42.3 us (2%)
  starting transfers between devices  24.4 us (1%)
    ppermute x19, waiting for transfers between devices, from_behind(): lax.ppermute(value, axis, [(source, source + steps) for source in range(i...  1150 us
    unnamed x4, waiting for transfers between devices  121 us
    another operation x4, local copies, waits for them, and re-layouts, effective_panel(): blocked = panel.reshape(panel.shape[0] // BLK, BLK, col_count, BLK)  78.6 us
    reshape x2, local copies, waits for them, and re-layouts, effective_panel(): return blocked.reshape(panel.shape)  45.1 us
    scatter-add x2, local copies, waits for them, and re-layouts, effective_panel(): blocked.at[blocks // col_count, :, blocks % col_count, :]  38.8 us
  transfers between devices with their start and end apart: 22, of which 21 were waited for; matrix products, arithmetic and copies ran while one was open for 5% of the time, Pallas kernels for 0%

commit v1 on v0

v1 whole, which is shorter than its diff:
```python
import functools

import jax
import jax.numpy as jnp
from jax import lax
from jax.experimental import pallas as pl
from jax.experimental.pallas import tpu as pltpu
from jax.sharding import PartitionSpec as P

BLK = 64
EPS = 1e-05
CHUNK = 16
WIDE = 512
MESH = pl.DeviceIdType.MESH


def meet(peers):
    barrier = pltpu.get_barrier_semaphore()
    for peer in peers:
        pl.semaphore_signal(barrier, inc=1, device_id=peer, device_id_type=MESH)
    pl.semaphore_wait(barrier, len(peers))


def share_tiles(dp_count, own_ref, all_ref, send_sems, recv_sems, own_sem):
    stage = lax.axis_index("pipe")
    me = lax.axis_index("dp")

    def peer(offset):
        return (stage, lax.rem(me + offset, dp_count))

    meet([peer(offset) for offset in range(1, dp_count)])

    def copy(offset):
        return pltpu.make_async_remote_copy(
            src_ref=own_ref,
            dst_ref=all_ref.at[me],
            send_sem=send_sems.at[offset],
            recv_sem=recv_sems.at[offset],
            device_id=peer(offset),
            device_id_type=MESH,
        )

    own = pltpu.make_async_copy(own_ref, all_ref.at[me], own_sem)
    own.start()
    copies = [copy(offset) for offset in range(1, dp_count)]
    for each in copies:
        each.start()
    own.wait()
    for each in copies:
        each.wait()


def chain(
    dp_count,
    pipe_count,
    value_in,
    output_in,
    first_in,
    gain_ref,
    upstream_ref,
    hidden_out,
    inverse,
    values_ref,
    back_ref,
    value_all,
    output_all,
    inbox,
    outbox,
    back_sum,
    ring_send,
    ring_recv,
    pair_send,
    pair_recv,
    hop_send,
    hop_recv,
    first_sem,
    keep_sem,
):
    stage = lax.axis_index("pipe")
    me = lax.axis_index("dp")
    ring = dp_count // 2
    half = ring // 2
    place = me // 2
    core = lax.rem(me, 2)
    value_rows = value_in.shape[0]
    output_rows = output_in.shape[0]
    width = output_in.shape[1]
    value_width = value_in.shape[1]
    chunk_count = inbox.shape[0]
    tokens = chunk_count * CHUNK
    wide_count = width // WIDE

    following = (lax.rem(stage + 1, pipe_count), me)
    previous = (lax.rem(stage + pipe_count - 1, pipe_count), me)
    near = [(stage, lax.rem(place + step, ring) * 2 + core) for step in (1, ring - 1)]
    meet(near + [(stage, place * 2 + 1 - core), following, previous])

    load_first = pltpu.make_async_copy(first_in, inbox, first_sem)

    @pl.when(stage == 0)
    def _():
        load_first.start()

    def slot(kind, index):
        if kind == 0:
            return value_all.at[pl.ds(pl.multiple_of(index * value_rows, value_rows), value_rows), :]
        return output_all.at[pl.ds(pl.multiple_of(index * output_rows, output_rows), output_rows), :]

    def at_distance(way, distance):
        step = -distance if way == 0 else distance
        return lax.rem(place + step + ring, ring) * 2 + core

    def ring_copy(way, kind, distance):
        index = at_distance(way, distance)
        source = slot(kind, index)
        if distance == 0:
            source = value_in if kind == 0 else output_in
        goal = lax.rem(place + (1 if way == 0 else ring - 1), ring) * 2 + core
        return pltpu.make_async_remote_copy(
            src_ref=source,
            dst_ref=slot(kind, index),
            send_sem=ring_send.at[way, kind, distance],
            recv_sem=ring_recv.at[way, kind, distance],
            device_id=(stage, goal),
            device_id_type=MESH,
        )

    def ring_arrival(way, kind, distance):
        index = at_distance(way, distance)
        return pltpu.make_async_remote_copy(
            src_ref=slot(kind, index),
            dst_ref=slot(kind, index),
            send_sem=ring_send.at[way, kind, distance - 1],
            recv_sem=ring_recv.at[way, kind, distance - 1],
            device_id=(stage, place * 2 + core),
            device_id_type=MESH,
        )

    def pair_copy(number, way, kind, distance):
        index = at_distance(way, distance)
        source = slot(kind, index)
        if distance == 0:
            source = value_in if kind == 0 else output_in
        return pltpu.make_async_remote_copy(
            src_ref=source,
            dst_ref=slot(kind, index),
            send_sem=pair_send.at[number],
            recv_sem=pair_recv.at[number],
            device_id=(stage, place * 2 + 1 - core),
            device_id_type=MESH,
        )

    def pair_arrival(number, way, kind, distance):
        step = -distance if way == 0 else distance
        index = lax.rem(place + step + ring, ring) * 2 + 1 - core
        return pltpu.make_async_remote_copy(
            src_ref=slot(kind, index),
            dst_ref=slot(kind, index),
            send_sem=pair_send.at[number],
            recv_sem=pair_recv.at[number],
            device_id=(stage, place * 2 + 1 - core),
            device_id_type=MESH,
        )

    def reach(way, kind):
        return half if way == kind else half - 1

    sent = []
    pairs = []
    arrivals = []

    def pass_on(way, kind, distance):
        number = len(pairs)
        copy = pair_copy(number, way, kind, distance)
        copy.start()
        pairs.append(copy)
        arrivals.append(pair_arrival(number, way, kind, distance))

    def send_on(way, kind, distance):
        if distance < reach(way, kind):
            copy = ring_copy(way, kind, distance)
            copy.start()
            sent.append(copy)

    for kind in (0, 1):
        for way in (0, 1):
            send_on(way, kind, 0)
    for kind in (0, 1):
        pass_on(0, kind, 0)
    value_all[pl.ds(pl.multiple_of(me * value_rows, value_rows), value_rows), :] = value_in[...]
    output_all[pl.ds(pl.multiple_of(me * output_rows, output_rows), output_rows), :] = output_in[...]
    for distance in range(1, half + 1):
        for kind in (0, 1):
            for way in (0, 1):
                if distance <= reach(way, kind):
                    ring_arrival(way, kind, distance).wait_recv()
                    send_on(way, kind, distance)
                    pass_on(way, kind, distance)
    for arrival in arrivals:
        arrival.wait_recv()

    def back_values():
        back_sum[...] = jnp.zeros_like(back_sum)

        @pl.loop(0, wide_count)
        def _(block):
            columns = pl.ds(pl.multiple_of(block * WIDE, WIDE), WIDE)
            back_sum[...] += lax.dot_general(
                upstream_ref[:, columns],
                output_all[:, columns],
                (((1,), (1,)), ((), ())),
                preferred_element_type=jnp.float32,
            )

        back_ref[...] = back_sum[...].astype(jnp.bfloat16)

    @pl.when(stage * 2 >= pipe_count)
    def _():
        back_values()

    @pl.when(stage == 0)
    def _():
        load_first.wait()

    def hop(index):
        return pltpu.make_async_remote_copy(
            src_ref=outbox.at[index],
            dst_ref=inbox.at[index],
            send_sem=hop_send.at[index],
            recv_sem=hop_recv.at[index],
            device_id=following,
            device_id_type=MESH,
        )

    @pl.loop(0, chunk_count)
    def _(index):
        @pl.when(stage > 0)
        def _():
            hop(index).wait_recv()

        squares = jnp.zeros((CHUNK, WIDE), jnp.float32)
        mixed = jnp.zeros((CHUNK, value_width), jnp.float32)
        for block in range(wide_count):
            columns = slice(block * WIDE, (block + 1) * WIDE)
            hidden = inbox[index, :, columns].astype(jnp.float32)
            squares = squares + hidden * hidden
            scaled = (hidden * gain_ref[:, columns]).astype(jnp.bfloat16)
            mixed = mixed + jnp.dot(
                scaled, value_all[columns, :], preferred_element_type=jnp.float32
            )
        scale = lax.rsqrt(jnp.sum(squares, axis=1, keepdims=True) / width + EPS)
        inverse[index] = jnp.broadcast_to(scale, (CHUNK, 128))
        values = (mixed * scale).astype(jnp.bfloat16)
        values_ref[index] = values

        @pl.when(stage < pipe_count - 1)
        def _():
            for block in range(wide_count):
                columns = slice(block * WIDE, (block + 1) * WIDE)
                added = jnp.dot(values, output_all[:, columns], preferred_element_type=jnp.float32)
                outbox[index, :, columns] = (
                    inbox[index, :, columns].astype(jnp.float32) + added
                ).astype(jnp.bfloat16)
            hop(index).start()

    @pl.when(stage * 2 < pipe_count)
    def _():
        back_values()

    keep = pltpu.make_async_copy(inbox, hidden_out, keep_sem)
    keep.start()
    for copy in sent + pairs:
        copy.wait_send()

    @pl.when(stage < pipe_count - 1)
    def _():
        @pl.loop(0, chunk_count)
        def _(index):
            hop(index).wait_send()

    keep.wait()


def tile_grads(
    value_blocks,
    output_blocks,
    hidden_ref,
    inverse,
    values_ref,
    back_ref,
    gain_ref,
    upstream_ref,
    partial,
):
    tokens, value_width = back_ref.shape
    width = upstream_ref.shape[1]
    value_cols = value_width // BLK
    output_cols = width // BLK
    lanes = lax.broadcasted_iota(jnp.int32, (BLK, 2 * BLK), 1)

    def pair_of(block):
        return pl.ds(pl.multiple_of(lax.div(block, 2) * (2 * BLK), 2 * BLK), 2 * BLK)

    def quadrant(product, row, turn):
        upper = jnp.where(lax.rem(row, 2) == 0, product[:BLK], product[BLK:])
        return jnp.where(turn == 1, pltpu.roll(upper, BLK, 1), upper)

    @pl.loop(0, partial.shape[0])
    def _(owner):
        for which in range(2):
            number = value_blocks[owner * 2 + which]
            row, column = lax.div(number, value_cols), lax.rem(number, value_cols)
            left = hidden_ref[:, :, pair_of(row)].astype(jnp.float32)
            left = left * inverse[...] * gain_ref[:, pair_of(row)]
            left = left.reshape(tokens, 2 * BLK).astype(jnp.bfloat16)
            product = lax.dot_general(
                left,
                back_ref[:, pair_of(column)],
                (((0,), (0,)), ((), ())),
                preferred_element_type=jnp.float32,
            )
            value_part = quadrant(product, row, lax.rem(column, 2))
            number = output_blocks[owner * 2 + which]
            row, column = lax.div(number, output_cols), lax.rem(number, output_cols)
            product = lax.dot_general(
                values_ref[:, :, pair_of(row)].reshape(tokens, 2 * BLK),
                upstream_ref[:, pair_of(column)],
                (((0,), (0,)), ((), ())),
                preferred_element_type=jnp.float32,
            )
            output_part = quadrant(product, row, 1 - lax.rem(column, 2))
            partial[owner, which] = jnp.where(lanes < BLK, value_part, output_part).astype(
                jnp.bfloat16
            )


def scatter_sum(dp_count, partial, grads_ref, landing, send_sems, recv_sems):
    stage = lax.axis_index("pipe")
    me = lax.axis_index("dp")

    def peer(offset):
        return (stage, lax.rem(me + offset, dp_count))

    meet([peer(offset) for offset in range(1, dp_count)])

    def copy(offset):
        return pltpu.make_async_remote_copy(
            src_ref=partial.at[lax.rem(me + offset, dp_count)],
            dst_ref=landing.at[offset],
            send_sem=send_sems.at[offset],
            recv_sem=recv_sems.at[offset],
            device_id=peer(offset),
            device_id_type=MESH,
        )

    copies = [copy(offset) for offset in range(1, dp_count)]
    for each in copies:
        each.start()
    total = partial[me].astype(jnp.float32)
    for offset, each in enumerate(copies, start=1):
        each.wait_recv()
        total = total + landing[offset].astype(jnp.float32)
    grads_ref[...] = total
    for each in copies:
        each.wait_send()


def shards(
    pipe_count,
    dp_count,
    first_input,
    section_gain,
    value_panel,
    output_panel,
    value_tiles,
    output_tiles,
    value_blocks,
    output_blocks,
    upstream,
):
    width = first_input.shape[2]
    tokens = first_input.shape[0] * first_input.shape[1]
    value_width = value_panel.shape[2]
    value_rows = value_panel.shape[1]
    output_rows = output_panel.shape[1]
    tile_count = value_blocks.shape[1]
    chunk_count = tokens // CHUNK
    me = lax.axis_index("dp")
    vmem = pl.BlockSpec(memory_space=pltpu.VMEM)
    smem = pl.BlockSpec(memory_space=pltpu.SMEM)
    hbm = pl.BlockSpec(memory_space=pl.ANY)
    dma = pltpu.SemaphoreType.DMA

    own = jnp.concatenate(
        [value_tiles.reshape(BLK, 2 * BLK), output_tiles.reshape(BLK, 2 * BLK)], axis=0
    )
    shared = pl.pallas_call(
        functools.partial(share_tiles, dp_count),
        out_shape=jax.ShapeDtypeStruct((dp_count, 2 * BLK, 2 * BLK), jnp.bfloat16),
        in_specs=[vmem],
        out_specs=vmem,
        scratch_shapes=[dma((dp_count,)), dma((dp_count,)), dma(())],
        compiler_params=pltpu.CompilerParams(collective_id=0, has_side_effects=True),
        name="share_tiles",
    )(own)
    shared = shared.reshape(dp_count, 2, 2, BLK * BLK)
    value_delta = shared[:, 0].reshape(tile_count, BLK * BLK)
    output_delta = shared[:, 1].reshape(tile_count, BLK * BLK)

    value_cols = value_width // BLK
    output_cols = width // BLK
    own_rows = value_rows // BLK
    wanted = me * (own_rows * value_cols) + jnp.arange(own_rows * value_cols)
    choose = (wanted[:, None] == value_blocks[0][None, :]).astype(jnp.bfloat16)
    placed = jnp.dot(choose, value_delta, preferred_element_type=jnp.float32)
    placed = placed.reshape(own_rows, value_cols, BLK, BLK).transpose(0, 2, 1, 3)
    value_eff = (
        value_panel[0].astype(jnp.float32) + placed.reshape(value_rows, value_width)
    ).astype(jnp.bfloat16)

    start = me * output_rows
    output_delta = output_delta.reshape(tile_count, BLK // output_rows, output_rows * BLK)
    output_delta = lax.dynamic_index_in_dim(
        output_delta, lax.rem(start, BLK) // output_rows, 1, keepdims=False
    )
    wanted = start // BLK * output_cols + jnp.arange(output_cols)
    choose = (wanted[:, None] == output_blocks[0][None, :]).astype(jnp.bfloat16)
    placed = jnp.dot(choose, output_delta, preferred_element_type=jnp.float32)
    placed = placed.reshape(output_cols, output_rows, BLK).transpose(1, 0, 2)
    output_eff = (
        output_panel[0].astype(jnp.float32) + placed.reshape(output_rows, width)
    ).astype(jnp.bfloat16)

    half = dp_count // 4
    hidden_shape = (chunk_count, CHUNK, width)
    upstream = upstream.reshape(tokens, width)
    hidden, inverse, values, value_back = pl.pallas_call(
        functools.partial(chain, dp_count, pipe_count),
        out_shape=[
            jax.ShapeDtypeStruct(hidden_shape, jnp.bfloat16),
            jax.ShapeDtypeStruct((chunk_count, CHUNK, 128), jnp.float32),
            jax.ShapeDtypeStruct((chunk_count, CHUNK, value_width), jnp.bfloat16),
            jax.ShapeDtypeStruct((tokens, value_width), jnp.bfloat16),
        ],
        in_specs=[vmem, vmem, hbm, vmem, vmem],
        out_specs=[hbm, vmem, vmem, vmem],
        scratch_shapes=[
            pltpu.VMEM((width, value_width), jnp.bfloat16),
            pltpu.VMEM((value_width, width), jnp.bfloat16),
            pltpu.VMEM(hidden_shape, jnp.bfloat16),
            pltpu.VMEM(hidden_shape, jnp.bfloat16),
            pltpu.VMEM((tokens, value_width), jnp.float32),
            dma((2, 2, half)),
            dma((2, 2, half)),
            dma((dp_count,)),
            dma((dp_count,)),
            dma((chunk_count,)),
            dma((chunk_count,)),
            dma(()),
            dma(()),
        ],
        compiler_params=pltpu.CompilerParams(
            collective_id=1, has_side_effects=True, vmem_limit_bytes=60 * 1024 * 1024
        ),
        name="chain",
    )(value_eff, output_eff, first_input.reshape(hidden_shape), section_gain, upstream)
    partial = pl.pallas_call(
        tile_grads,
        out_shape=jax.ShapeDtypeStruct((dp_count, 2, BLK, 2 * BLK), jnp.bfloat16),
        in_specs=[smem, smem] + [vmem] * 6,
        out_specs=vmem,
        compiler_params=pltpu.CompilerParams(vmem_limit_bytes=32 * 1024 * 1024),
        name="tile_grads",
    )(value_blocks[0], output_blocks[0], hidden, inverse, values, value_back, section_gain, upstream)
    grads = pl.pallas_call(
        functools.partial(scatter_sum, dp_count),
        out_shape=jax.ShapeDtypeStruct((2, BLK, 2 * BLK), jnp.float32),
        in_specs=[vmem],
        out_specs=vmem,
        scratch_shapes=[
            pltpu.VMEM((dp_count, 2, BLK, 2 * BLK), jnp.bfloat16),
            dma((dp_count,)),
            dma((dp_count,)),
        ],
        compiler_params=pltpu.CompilerParams(collective_id=2, has_side_effects=True),
        name="scatter_sum",
    )(partial)
    value_grads = grads[:, :, :BLK].reshape(1, 2, BLK * BLK)
    output_grads = grads[:, :, BLK:].reshape(1, 2, BLK * BLK)
    return (value_grads, output_grads)


def solution(mesh):
    in_specs = (
        P(None, "dp", None),
        P("pipe", None),
        P("pipe", "dp", None),
        P("pipe", "dp", None),
        P("pipe", "dp", None),
        P("pipe", "dp", None),
        P("pipe", None),
        P("pipe", None),
        P("pipe", None, "dp", None),
    )
    out_specs = (P("pipe", "dp", None), P("pipe", "dp", None))
    body = functools.partial(shards, mesh.shape["pipe"], mesh.shape["dp"])
    return jax.shard_map(body, mesh=mesh, in_specs=in_specs, out_specs=out_specs, check_vma=False)
```

time: 1790 us -> 396 us (0.22)
  waiting for transfers between devices: 1280 us -> 0 us
  Pallas kernels: 0 us -> 370 us
  local copies, waits for them, and re-layouts: 285 us -> 17.4 us
  matrix products: 84.3 us -> 1.89 us
  blocking collectives: 42.3 us -> 0 us
  other arithmetic: 43.8 us -> 4.59 us
  starting transfers between devices: 24.4 us -> 0 us
    ppermute x19 -> x0, waiting for transfers between devices: 1150 us -> none  [from_behind(): lax.ppermute(value, axis, [(source, source + steps) for source in range(i...]
    pallas_call x0 -> x4, Pallas kernels: none -> 370 us  [the longest x1 320 us: shards(): pl.pallas_call(functools.partial(chain, dp_count, pipe_count), out_shape=...]
    unnamed x4 -> x0, waiting for transfers between devices: 121 us -> none
    reshape x42 -> x7, local copies, waits for them, and re-layouts: 112 us -> 5.2 us  [the longest x1 1.16 us: shards(): shared = shared.reshape(dp_count, 2, 2, BLK * BLK)]
    another operation x24 -> x2, local copies, waits for them, and re-layouts: 98 us -> 0.3 us  [the longest x1 0.2 us: shards(): output_delta.reshape(tile_count, BLK // output_rows, output_rows * BLK)]
    dot_general x20 -> x2, matrix products: 84.3 us -> 1.89 us  [the longest x1 1.53 us: shards(): placed = jnp.dot(choose, value_delta, preferred_element_type=jnp.float32)]
    all_gather x2 -> x0, blocking collectives: 42.3 us -> none  [the longest x1 23.3 us: shards(): lax.all_gather(value_tiles, 'dp', axis=1, tiled=True)]
    scatter-add x2 -> x0, local copies, waits for them, and re-layouts: 38.8 us -> none  [effective_panel(): blocked.at[blocks // col_count, :, blocks % col_count, :]]
  transfers between devices with their start and end apart: 22 -> 0, of which waited for: 21 -> 0; matrix products, arithmetic and copies ran while one was open for 5% -> 0% of each run, Pallas kernels for 0% -> 0%
where the time goes in v1:
time: 396 us; the launch traced here: 395 us
  Pallas kernels  370 us (93%)
  local copies, waits for them, and re-layouts  17.4 us (4%)
  other arithmetic  4.59 us (1%)
    pallas_call x1, Pallas kernels, shards(): pl.pallas_call(functools.partial(chain, dp_count, pipe_count), out_shape=...  320 us
    pallas_call x1, Pallas kernels, shards(): pl.pallas_call(functools.partial(share_tiles, dp_count), out_shape=jax.Sh...  22.3 us
    pallas_call x1, Pallas kernels, shards(): pl.pallas_call(functools.partial(scatter_sum, dp_count), out_shape=jax.Sh...  21.2 us
    unnamed x20, local copies, waits for them, and re-layouts  8.49 us

profile of v1, /device:TPU:31, one launch (start us, length us, event | category | flops | bytes accessed | tf_op | source)
XLA Modules:
  0.0 395.0 jit_solution(12222961013840466731)
XLA Ops:
  0.7 0.7 reshape.61
  1.4 0.7 reshape.62
  2.2 0.6 pad_maximum_fusion.own_ref
  2.8 22.3 %share_tiles.1 = bf16[16,128,128]{2,1,0:T(8,128)(2,1)} custom-call(bf16[128,128]{1,0:T(8,128)(2,1)} %pad_maximum_fusion.own_ref), custom_call_target="tpu_custom_call" | custom-call | tf_op jit(solution)/shard_map/share_tiles/pallas_call | solution.py:397
  25.1 1.2 reshape.63
  27.7 1.3 dot_general.15
  29.4 0.6 copy.18
  30.0 0.7 reshape.65
  30.7 2.0 fusion.output_in
  32.6 1.5 convolution_bitcast_fusion
  34.2 0.5 reshape.64
  34.7 2.0 fusion.1.value_in
  36.7 320.0 %chain.1 = (bf16[16,16,8192]{2,1,0:T(8,128)(2,1)}, f32[16,16,128]{2,1,0:T(8,128)}, bf16[16,16,512]{2,1,0:T(8,128)(2,1)}, bf16[256,512]{1,0:T(8,128)(2,1)}) custom-call(bf16[512,512]{1,0:T(8,128)(2,1)} %fusion.1.value_in, bf16[32,8192]{1,0:T(8,128)(2,1)} %fusion.output_in, bf16[16,16,8192]{2,1,0:T(8,128)(2,1)} %bitcast.47, f32[1,8192]{1,0:T(1,128)} %gain_ref.3, ...), custom_call_target="tpu_custom_call" | custom-call | tf_op jit(solution)/shard_map/chain/pallas_call | solution.py:437
  356.7 2.2 copy-done
  358.9 2.2 copy-done.1
  361.1 0.9 copy-done.3
  362.1 0.9 copy-done.4
  363.0 0.9 copy-done.5
  363.9 6.7 %tile_grads.1.partial = bf16[16,2,64,128]{3,2,1,0:T(8,128)(2,1)S(1)} custom-call(s32[32]{0:T(128)S(1)} %bitcast.46, s32[32]{0:T(128)S(1)} %bitcast.44, bf16[16,16,8192]{2,1,0:T(8,128)(2,1)S(1)} %copy-done.1, f32[16,16,128]{2,1,0:T(8,128)S(1)} %copy-done.5, bf16[16,16,512]{2,1,0:T(8,128)(2,1)S(1)} %copy-done.3, bf16[256,512]{1,0:T(8,128)(2,1)S(1)} %copy-done.4, ...), custom_call_target="tpu_custom_call" | custom-call | tf_op jit(solution)/shard_map/tile_grads/pallas_call | solution.py:467
  370.6 0.8 copy-done.2
  371.4 21.2 %scatter_sum.1 = f32[2,64,128]{2,1,0:T(8,128)} custom-call(bf16[16,2,64,128]{3,2,1,0:T(8,128)(2,1)} %copy-done.2), custom_call_target="tpu_custom_call" | custom-call | tf_op jit(solution)/shard_map/scatter_sum/pallas_call | solution.py:475
  392.6 1.0 fusion.13
  393.6 0.7 reshape.69
  394.3 0.7 reshape.68
  (21 shorter events, 1.7 us)
Async XLA Ops:
  0.6 28.4 %copy-start.7 = (s32[1,32]{1,0:T(1,128)S(1)}, s32[1,32]{1,0:T(1,128)}, u32[]{:S(2)}) copy-start(s32[1,32]{1,0:T(1,128)} %param.16) | copy-start | bytes 388
  29.4 3.2 copy-start.8
  36.7 320.1 %copy-start.6 = (f32[1,8192]{1,0:T(1,128)S(1)}, f32[1,8192]{1,0:T(1,128)}, u32[]{:S(2)}) copy-start(f32[1,8192]{1,0:T(1,128)} %gain_ref.3) | copy-start | bytes 98308
  356.7 2.2 copy-start
  358.9 2.2 copy-start.1
  361.1 0.9 copy-start.3
  362.0 0.9 copy-start.4
  363.0 0.9 copy-start.5
  370.6 0.8 copy-start.2
